TPU v7x, 32 devices: a whole 2x2x4 slice. The times are simulated.
32 devices in a mesh: blk: 8 (over z, y), hid: 4 (over x, core).
Axes of the slice: x: 2, y: 2, z: 4, core: 2. Of those that a mesh axis runs over, the one named last changes fastest.
Arguments:
- queries: bfloat16 [768, 128], P('blk'), may hold values from -6 to 6
- node_table: bfloat16 [65536, 128], P('blk'), may hold values from -6 to 6
- beam: int32 [768, 128], P('blk'), may hold values from 0 to 65535, as said below
- w_query: bfloat16 [128, 256], P(None, 'hid'), may hold values from -0.5 to 0.5
- w_node: bfloat16 [128, 256], P(None, 'hid'), may hold values from -0.5 to 0.5
- w_cross: bfloat16 [128, 256], P(None, 'hid'), may hold values from -0.5 to 0.5
- bias_hidden: bfloat16 [256], P('hid'), may hold values from -3 to 3
- w_out: bfloat16 [256], P('hid'), may hold values from -0.375 to 0.375
Outputs:
- scores: float32 [768, 128], P('blk', 'hid')
Inputs may be any that keep to these rules, and one draw needn't show every extreme that they name: `beam`: each query's entries are distinct and come in sibling pairs 2p, 2p + 1 of 64 parents. Among the rows of one blk index (96 queries) at most 3072 entries lie in any one aligned range of 8192 nodes, and some range holds exactly 3072.
All inputs are finite; a program needn't handle non-finite values.
Results may differ from a plain program's by a relative error of at most 0.007.
Values may be sent and summed in bfloat16 or wider, within the bound.
No kernel may reach another device: no remote copies, remote signals or barrier semaphores. Data moves between devices by JAX's collectives and lax.ppermute only.
A program may use at most 64 MiB of HBM per device.

v0:
```python
import functools

import jax
import jax.numpy as jnp
from jax import lax
from jax.experimental import pallas as pl
from jax.experimental.pallas import tpu as pltpu
from jax.sharding import PartitionSpec as P


SLOT = 8
KIDS = 2 * SLOT
READY = 2
FIELD = 20
SHIFT = 8
LANES = 128
SUBLANES = 8
TAIL = 16

VMEM = pl.BlockSpec(memory_space=pltpu.VMEM)


def prepare_kernel(part, table_ref, *refs):
    packs = refs[:-5]
    wide_ref, mix_ref, first_ref, column_ref, bias_ref = refs[-5:]
    feat = table_ref.shape[1]

    @pl.when(pl.program_id(0) == 0)
    def _():
        stacked = [
            jnp.concatenate([p[i * part : (i + 1) * part, :] for p in packs], axis=0)
            for i in range(3)
        ]
        first_ref[...] = stacked[0].T
        mix_ref[0:feat, :] = stacked[1].T
        mix_ref[feat:, :] = stacked[2].T
        ends = [p[3 * part :, :].astype(jnp.float32) for p in packs]
        out_row = jnp.concatenate([e[0:1, 0:part] for e in ends], axis=1)
        bias = jnp.concatenate([e[1:2, 0:part] for e in ends], axis=1)
        column_ref[...] = (
            jnp.broadcast_to(out_row, (feat, out_row.shape[1])).T.astype(jnp.bfloat16)
        )
        bias_ref[...] = jnp.broadcast_to(bias, bias_ref.shape)

    wide_ref[...] = table_ref[...].astype(jnp.float32)


def prepare(table, packs):
    rows, width = table.shape
    block = min(rows, 2048)
    part = (packs[0].shape[0] - TAIL) // 3
    hidden = part * len(packs)
    whole = lambda shape: pl.BlockSpec(shape, lambda i: (0, 0))
    shapes = ((2 * width, hidden), (width, hidden), (hidden, width), (SUBLANES, hidden))
    types = (jnp.bfloat16, jnp.bfloat16, jnp.bfloat16, jnp.float32)
    return pl.pallas_call(
        functools.partial(prepare_kernel, part),
        grid=(rows // block,),
        in_specs=[pl.BlockSpec((block, width), lambda i: (i, 0))]
        + [whole(packs[0].shape)] * len(packs),
        out_specs=(pl.BlockSpec((block, width), lambda i: (i, 0)), *[whole(x) for x in shapes]),
        out_shape=(
            jax.ShapeDtypeStruct((rows, width), jnp.float32),
            *[jax.ShapeDtypeStruct(x, t) for x, t in zip(shapes, types)],
        ),
        compiler_params=pltpu.CompilerParams(vmem_limit_bytes=12 * 2**20),
        cost_estimate=pl.CostEstimate(flops=0, bytes_accessed=6 * rows * width, transcendentals=0),
    )(table, *packs)


def score_kernel(shard_rows, digits, tile_queries, follows, *refs):
    asked_ref, table_ref, mix_ref, first_ref, column_ref, bias_ref = refs[:6]
    (
        out_ref,
        sum_ref,
        query_ref,
        start_ref,
        key_ref,
        need_ref,
        flat_ref,
        total_ref,
        found_ref,
        place_ref,
        done,
    ) = refs[6 + follows :]
    width, rows = out_ref.shape
    feat = table_ref.shape[1]
    hidden_width = mix_ref.shape[1]
    tile = tile_queries * KIDS
    tiles = rows // tile_queries
    limit = width // 2 // SLOT

    ids = asked_ref[rows : 2 * rows, :].astype(jnp.int32)
    for d in range(2, digits + 1):
        ids = (ids << SHIFT) + asked_ref[d * rows : (d + 1) * rows, :].astype(jnp.int32)
    local = ids - lax.axis_index("blk") * shard_rows
    owned = (local >= 0) & (local < shard_rows)
    even = owned & ((local & 1) == 0)
    lane = lax.broadcasted_iota(jnp.int32, (rows, width), 1)
    earlier = (
        lax.broadcasted_iota(jnp.int32, (width, width), 0)
        < lax.broadcasted_iota(jnp.int32, (width, width), 1)
    ).astype(jnp.bfloat16)
    even_count = even.astype(jnp.float32)
    rank = jnp.dot(even_count.astype(jnp.bfloat16), earlier, preferred_element_type=jnp.float32)
    shift = lane - rank.astype(jnp.int32)
    word = jnp.where(even, (local >> 1) + (shift << FIELD) + (1 << (FIELD + 8)), 0)
    hop = 1
    while hop < width:
        bit = hop << FIELD
        moved = pltpu.roll(word, width - hop, 1)
        word = jnp.where((moved & bit) != 0, moved, jnp.where((word & bit) != 0, 0, word))
        hop *= 2
    front = word & ((1 << FIELD) - 1)
    slots = (front * 2).T
    for c in range(limit):
        flat_ref[c, :, 0:rows] = slots[c * SLOT : (c + 1) * SLOT, :]
    ahead = pltpu.make_async_copy(
        flat_ref.at[pl.ds(0, READY)], place_ref.at[pl.ds(0, READY)], done.at[0]
    )
    ahead.start()
    most = jnp.max(jnp.sum(even_count, axis=1, keepdims=True)).astype(jnp.int32)
    passes = (most + (SLOT - 1)) // SLOT
    need_ref[...] = jnp.where(word != 0, front, -1)
    key_ref[...] = jnp.where(owned, local, -4)
    queries = asked_ref[0:rows, :]
    query_ref[...] = queries.astype(jnp.float32)
    start_ref[...] = (
        jnp.dot(queries, first_ref[...], preferred_element_type=jnp.float32) + bias_ref[0:1, :]
    )
    sum_ref[...] = (
        lax.broadcasted_iota(jnp.int32, (tile_queries, tile), 1) // KIDS
        == lax.broadcasted_iota(jnp.int32, (tile_queries, tile), 0)
    ).astype(jnp.bfloat16)
    total_ref[...] = jnp.zeros(total_ref.shape, jnp.float32)
    ahead.wait()

    def gather(block, k):
        for i in range(tile_queries):
            for t in range(SLOT):
                at = pl.multiple_of(place_ref[block, t, k * tile_queries + i], 2)
                found_ref[k, pl.ds(i * KIDS + 2 * t, 2), :] = table_ref[pl.ds(at, 2), :]

    def score(c, k):
        some = slice(k * tile_queries, (k + 1) * tile_queries)
        nodes = found_ref[k]
        spread = jnp.broadcast_to(query_ref[some, :][:, None, :], (tile_queries, KIDS, feat))
        crossed = (nodes * spread.reshape(tile, feat)).astype(jnp.bfloat16)
        joined = jnp.concatenate([nodes.astype(jnp.bfloat16), crossed], axis=1)
        pre = jnp.dot(joined, mix_ref[...], preferred_element_type=jnp.float32)
        pre = pre.reshape(tile_queries, KIDS, hidden_width) + start_ref[some, :][:, None, :]
        hidden = jnp.maximum(pre.reshape(tile, hidden_width).astype(jnp.bfloat16), 0)
        score = jnp.dot(hidden, column_ref[...], preferred_element_type=jnp.float32)
        need = need_ref[some, :]
        if isinstance(c, int):
            need = need[:, c * SLOT : (c + 1) * SLOT]
        else:
            need = pltpu.roll(need, (width - c * SLOT) % width, 1)
        key = key_ref[some, :]
        above = key >> 1
        parity = key & 1
        code = jnp.full((tile_queries, width), -1, jnp.int32)
        for t in range(SLOT):
            code = jnp.where(above == need[:, t : t + 1], 2 * t + parity, code)
        slot = lax.broadcasted_iota(jnp.int32, (tile_queries, KIDS, width), 1)
        hit = code[:, None, :] == slot
        hits = jnp.where(hit, score.reshape(tile_queries, KIDS, width), 0.0)
        total_ref[some, :] += jnp.dot(
            sum_ref[...],
            hits.reshape(tile, width).astype(jnp.bfloat16),
            preferred_element_type=jnp.float32,
        )

    def one_pass(c, block):
        gather(block, 0)
        for k in range(tiles):
            if k + 1 < tiles:
                gather(block, k + 1)
            score(c, k)

    for c in range(READY):
        pl.when(passes > c)(functools.partial(one_pass, c, c))

    def later(c, carry):
        copy = pltpu.make_async_copy(flat_ref.at[c], place_ref.at[READY], done.at[1])
        copy.start()
        copy.wait()
        one_pass(c, READY)
        return carry

    lax.fori_loop(READY, passes, later, 0)
    out_ref[...] = total_ref[...].T.astype(out_ref.dtype)


def score_source(asked, rows, shard_rows, prepared, before):
    wide, mix, first, column, bias = prepared
    feat = asked.shape[1]
    hidden, width = column.shape
    digits = asked.shape[0] // rows - 1
    tile_queries = next(n for n in (32, 24, 16, 8) if rows % n == 0)
    tile = tile_queries * KIDS
    lanes = -(-rows // LANES) * LANES
    return pl.pallas_call(
        functools.partial(score_kernel, shard_rows, digits, tile_queries, len(before)),
        in_specs=[VMEM] * 6 + [pl.BlockSpec(memory_space=pl.ANY)] * len(before),
        out_specs=VMEM,
        out_shape=jax.ShapeDtypeStruct((width, rows), jnp.bfloat16),
        scratch_shapes=[
            pltpu.VMEM((tile_queries, tile), jnp.bfloat16),
            pltpu.VMEM((rows, feat), jnp.float32),
            pltpu.VMEM((rows, hidden), jnp.float32),
            pltpu.VMEM((rows, width), jnp.int32),
            pltpu.VMEM((rows, width), jnp.int32),
            pltpu.VMEM((width // 2 // SLOT, SLOT, lanes), jnp.int32),
            pltpu.VMEM((rows, width), jnp.float32),
            pltpu.VMEM((rows // tile_queries, tile, feat), jnp.float32),
            pltpu.SMEM((READY + 1, SLOT, lanes), jnp.int32),
            pltpu.SemaphoreType.DMA((2,)),
        ],
        compiler_params=pltpu.CompilerParams(vmem_limit_bytes=16 * 2**20),
        cost_estimate=pl.CostEstimate(
            flops=2 * rows * KIDS * 3 * feat * hidden,
            bytes_accessed=4 * rows * KIDS * feat,
            transcendentals=0,
        ),
    )(asked, wide, mix, first, column, bias, *before)


def mirrored(value, count):
    result = 0
    while count > 1:
        result = result * 2 + value % 2
        value //= 2
        count //= 2
    return result


def shards(queries, node_table, beam, w_query, w_node, w_cross, bias_hidden, w_out):
    groups = lax.axis_size("blk")
    parts = lax.axis_size("hid")
    rows, width = beam.shape
    feat = queries.shape[1]
    shard_rows = node_table.shape[0]
    binary = groups & (groups - 1) == 0 and parts & (parts - 1) == 0
    turns = groups // parts

    def far(value, back=False):
        pairs = []
        for b in range(groups):
            for h in range(parts):
                k = (mirrored(h, parts) if binary else h) * turns
                to = b ^ k if binary else (b + k if back else b - k) % groups
                pairs.append((b * parts + h, to * parts + h))
        return lax.ppermute(value, ("blk", "hid"), pairs)

    def near(value, turn, back=False):
        pairs = [
            (b, b ^ turn if binary else (b + turn if back else b - turn) % groups)
            for b in range(groups)
        ]
        return lax.ppermute(value, "blk", pairs)

    def across(value, step):
        pairs = [(h, h ^ step if binary else (h + step) % parts) for h in range(parts)]
        return lax.ppermute(value, "hid", pairs)

    digits = -(-(groups * shard_rows - 1).bit_length() // SHIFT)
    split = [
        ((beam >> (SHIFT * d)) & (2**SHIFT - 1)).astype(queries.dtype)
        for d in reversed(range(digits))
    ]
    first = far(jnp.concatenate([queries] + split, axis=0))

    part = w_out.shape[0]
    ends = jnp.stack([w_out, bias_hidden])
    ends = jnp.pad(ends, ((0, TAIL - 2), (0, feat - part)))
    weights = jnp.concatenate([w_query.T, w_node.T, w_cross.T, ends], axis=0)
    packs = [weights] + [across(weights, step) for step in range(1, parts)]
    prepared = prepare(node_table, packs)

    total, before = None, ()
    for turn in reversed(range(turns)):
        asked = near(first, turn) if turn else first
        scored = score_source(asked, rows, shard_rows, prepared, before)
        before = (scored,)
        back = (near(scored, turn, True) if turn else scored).astype(jnp.float32)
        total = back if total is None else total + back
    total = far(total.astype(jnp.bfloat16), True)

    own = lax.axis_index("hid")
    piece = width // parts
    result = lax.dynamic_slice_in_dim(total, own * piece, piece, axis=0).astype(jnp.float32)
    for step in range(1, parts):
        peer = own ^ step if binary else (own + step) % parts
        sent = lax.dynamic_slice_in_dim(total, peer * piece, piece, axis=0)
        result = result + across(sent, step).astype(jnp.float32)
    return result.T


def solution(mesh):
    in_specs = (
        P("blk", None),
        P("blk", None),
        P("blk", None),
        P(None, "hid"),
        P(None, "hid"),
        P(None, "hid"),
        P("hid"),
        P("hid"),
    )
    out_specs = P("blk", "hid")
    return jax.shard_map(shards, mesh=mesh, in_specs=in_specs, out_specs=out_specs, check_vma=False)
```

profile of v0, /device:TPU:0, one launch (start us, length us, event | category | flops | bytes accessed | tf_op | source)
XLA Modules:
  0.0 37.8 jit_solution(18322829593101648541)
XLA Ops:
  0.0 0.8 %and_convert_fusion.1 = (bf16[96,128]{1,0:T(8,128)(2,1)S(1)}, bf16[96,128]{1,0:T(8,128)(2,1)S(1)}) fusion(s32[96,128]{1,0:T(8,128)} %param.10), kind=kLoop, calls=%fused_computation.4 | loop fusion | flops 73728 | bytes 98304 | tf_op jit(solution)/shard_map/convert_element_type | solution.py:269
  0.8 0.7 %pad_maximum_fusion = bf16[288,128]{1,0:T(8,128)(2,1)S(1)} fusion(bf16[96,128]{1,0:T(8,128)(2,1)S(1)} %get-tuple-element.16, bf16[96,128]{1,0:T(8,128)(2,1)S(1)} %get-tuple-element.15, bf16[96,128]{1,0:T(8,128)(2,1)} %param.8), kind=kLoop, calls=%fused_computation | loop fusion | flops 221184 | bytes 147456 | tf_op jit(solution)/shard_map/concatenate | solution.py:272
  1.6 0.7 %collective-permute-start = (bf16[288,128]{1,0:T(8,128)(2,1)S(1)}, bf16[288,128]{1,0:T(8,128)(2,1)S(1)}, u32[]{:S(2)}, u32[]{:S(2)}) collective-permute-start(bf16[288,128]{1,0:T(8,128)(2,1)S(1)} %pad_maximum_fusion), channel_id=1, source_target_pairs={{0,0},{1,17},{2,10},{3,27},{4,4},{5,21},{6,14},{7,31},{8,8},{9,25}... | collective-permute-start | bytes 221192 | tf_op jit(solution)/shard_map/ppermute | solution.py:254
  2.2 0.7 %fusion.5 = bf16[16,128]{1,0:T(8,128)(2,1)S(1)} fusion(bf16[1,64]{1,0:T(2,128)(2,1)} %bitcast.10, bf16[1,64]{1,0:T(2,128)(2,1)} %bitcast.11), kind=kLoop, calls=%fused_computation.13 | loop fusion | flops 22528 | bytes 4352 | tf_op jit(solution)/shard_map/stack | solution.py:275
  2.9 0.0 collective-permute-done.refs_0_
  2.9 3.1 %collective-permute-start.1 = (bf16[288,128]{1,0:T(8,128)(2,1)S(1)}, bf16[288,128]{1,0:T(8,128)(2,1)S(1)}, u32[]{:S(2)}, u32[]{:S(2)}) collective-permute-start(bf16[288,128]{1,0:T(8,128)(2,1)S(1)} %collective-permute-done.refs_0_), channel_id=1, source_target_pairs={{0,4},{4,0},{8,12},{12,8},{16,20},{20,16},{24,28},{28,24},{1,5},{5... | collective-permute-start | bytes 221192 | tf_op jit(solution)/shard_map/ppermute | solution.py:261
  6.0 0.8 %pad_maximum_fusion.1.refs_0_ = bf16[208,128]{1,0:T(8,128)(2,1)S(1)} fusion(bf16[16,128]{1,0:T(8,128)(2,1)S(1)} %fusion.5, bf16[64,128]{1,0:T(8,128)(2,1)} %bitcast.7, bf16[64,128]{1,0:T(8,128)(2,1)} %bitcast.8, bf16[64,128]{1,0:T(8,128)(2,1)} %bitcast.9), kind=kLoop, calls=%fused_computation.2 | loop fusion | flops 212992 | bytes 106496 | tf_op jit(solution)/shard_map/concatenate | solution.py:277
  6.7 4.1 %collective-permute-start.2 = (bf16[208,128]{1,0:T(8,128)(2,1)S(1)}, bf16[208,128]{1,0:T(8,128)(2,1)S(1)}, u32[]{:S(2)}, u32[]{:S(2)}) collective-permute-start(bf16[208,128]{1,0:T(8,128)(2,1)S(1)} %pad_maximum_fusion.1.refs_0_), channel_id=1, source_target_pairs={{0,1},{1,0},{2,3},{3,2},{4,5},{5,4},{6,7},{7,6},{8,9},{9,8},{10,11... | collective-permute-start | bytes 159752 | tf_op jit(solution)/shard_map/ppermute | solution.py:265
  10.9 2.5 %collective-permute-start.3 = (bf16[208,128]{1,0:T(8,128)(2,1)S(1)}, bf16[208,128]{1,0:T(8,128)(2,1)S(1)}, u32[]{:S(2)}, u32[]{:S(2)}) collective-permute-start(bf16[208,128]{1,0:T(8,128)(2,1)S(1)} %pad_maximum_fusion.1.refs_0_), channel_id=1, source_target_pairs={{0,2},{1,3},{2,0},{3,1},{4,6},{5,7},{6,4},{7,5},{8,10},{9,11},{10,... | collective-permute-start | bytes 159752 | tf_op jit(solution)/shard_map/ppermute | solution.py:265
  13.4 2.2 %collective-permute-done.3.refs_2_ = bf16[208,128]{1,0:T(8,128)(2,1)S(1)} collective-permute-done((bf16[208,128]{1,0:T(8,128)(2,1)S(1)}, bf16[208,128]{1,0:T(8,128)(2,1)S(1)}, u32[]{:S(2)}, u32[]{:S(2)}) %collective-permute-start.3) | collective-permute-done | bytes 53280 | tf_op jit(solution)/shard_map/ppermute | solution.py:265
  15.6 1.9 %collective-permute-done.4.refs_3_ = bf16[208,128]{1,0:T(8,128)(2,1)S(1)} collective-permute-done((bf16[208,128]{1,0:T(8,128)(2,1)S(1)}, bf16[208,128]{1,0:T(8,128)(2,1)S(1)}, u32[]{:S(2)}, u32[]{:S(2)}) %collective-permute-start.4) | collective-permute-done | bytes 53280 | tf_op jit(solution)/shard_map/ppermute | solution.py:265
  17.4 1.6 %copy-done = bf16[8192,128]{1,0:T(8,128)(2,1)S(1)} copy-done((bf16[8192,128]{1,0:T(8,128)(2,1)S(1)}, bf16[8192,128]{1,0:T(8,128)(2,1)}, u32[]{:S(2)}) %copy-start) | copy-done | bytes 2097176
  19.0 0.5 %shard_map.82 = (f32[8192,128]{1,0:T(8,128)S(1)}, bf16[256,256]{1,0:T(8,128)(2,1)S(1)}, bf16[128,256]{1,0:T(8,128)(2,1)S(1)}, bf16[256,128]{1,0:T(8,128)(2,1)S(1)}, f32[8,256]{1,0:T(8,128)S(1)}) custom-call(bf16[8192,128]{1,0:T(8,128)(2,1)S(1)} %copy-done, bf16[208,128]{1,0:T(8,128)(2,1)S(1)} %pad_maximum_fusion.1.refs_0_, ...), custom_call_target="tpu_custom_call" | custom-call | bytes 6291456 | tf_op jit(solution)/shard_map/pallas_call | solution.py:56
  19.5 0.0 collective-permute-done.1.refs_0_
  19.5 2.8 %shard_map.83.refs_6_ = bf16[128,96]{1,0:T(8,128)(2,1)S(1)} custom-call(bf16[288,128]{1,0:T(8,128)(2,1)S(1)} %collective-permute-done.1.refs_0_, f32[8192,128]{1,0:T(8,128)S(1)} %get-tuple-element.10.refs_1_, bf16[256,256]{1,0:T(8,128)(2,1)S(1)} %get-tuple-element.11.refs_2_, bf16[128,256]{1,0:T(8,128)(2,1)S(1)} %get-tuple-element.12.refs_3_, ...), custom_call_target="tpu_custom_call" | custom-call | flops 301989888 | bytes 786432 | tf_op jit(solution)/shard_map/pallas_call | solution.py:203
  22.3 0.6 %collective-permute-start.5 = (bf16[128,96]{1,0:T(8,128)(2,1)S(1)}, bf16[128,96]{1,0:T(8,128)(2,1)S(1)}, u32[]{:S(2)}, u32[]{:S(2)}) collective-permute-start(bf16[128,96]{1,0:T(8,128)(2,1)S(1)} %shard_map.83.refs_6_), channel_id=1, source_target_pairs={{0,4},{4,0},{8,12},{12,8},{16,20},{20,16},{24,28},{28,24},{1,5},{5... | collective-permute-start | bytes 73736 | tf_op jit(solution)/shard_map/ppermute | solution.py:261
  22.9 2.8 %shard_map.84 = bf16[128,96]{1,0:T(8,128)(2,1)S(1)} custom-call(bf16[288,128]{1,0:T(8,128)(2,1)S(1)} %collective-permute-done.refs_0_, f32[8192,128]{1,0:T(8,128)S(1)} %get-tuple-element.10.refs_1_, bf16[256,256]{1,0:T(8,128)(2,1)S(1)} %get-tuple-element.11.refs_2_, bf16[128,256]{1,0:T(8,128)(2,1)S(1)} %get-tuple-element.12.refs_3_, ...), custom_call_target="tpu_custom_call" | custom-call | flops 301989888 | bytes 786432 | tf_op jit(solution)/shard_map/pallas_call | solution.py:203
  25.7 0.6 %collective-permute-done.5 = bf16[128,96]{1,0:T(8,128)(2,1)S(1)} collective-permute-done((bf16[128,96]{1,0:T(8,128)(2,1)S(1)}, bf16[128,96]{1,0:T(8,128)(2,1)S(1)}, u32[]{:S(2)}, u32[]{:S(2)}) %collective-permute-start.5) | collective-permute-done | bytes 24608 | tf_op jit(solution)/shard_map/ppermute | solution.py:261
  26.3 0.7 %collective-permute-start.6 = (bf16[128,96]{1,0:T(8,128)(2,1)S(1)}, bf16[128,96]{1,0:T(8,128)(2,1)S(1)}, u32[]{:S(2)}, u32[]{:S(2)}) collective-permute-start(bf16[128,96]{1,0:T(8,128)(2,1)S(1)} %add_convert_fusion), channel_id=1, source_target_pairs={{0,0},{1,17},{2,10},{3,27},{4,4},{5,21},{6,14},{7,31},{8,8},{9,25}... | collective-permute-start | bytes 73736 | tf_op jit(solution)/shard_map/ppermute | solution.py:254
  27.0 4.9 %collective-permute-start.7 = (bf16[32,96]{1,0:T(8,128)(2,1)S(1)}, bf16[32,96]{1,0:T(8,128)(2,1)S(1)}, u32[]{:S(2)}, u32[]{:S(2)}) collective-permute-start(bf16[32,96]{1,0:T(8,128)(2,1)S(1)} %get-tuple-element.17), channel_id=1, source_target_pairs={{0,1},{1,0},{2,3},{3,2},{4,5},{5,4},{6,7},{7,6},{8,9},{9,8},{10,11... | collective-permute-start | bytes 18440 | tf_op jit(solution)/shard_map/ppermute | solution.py:265
  31.9 2.2 %collective-permute-start.8 = (bf16[32,96]{1,0:T(8,128)(2,1)S(1)}, bf16[32,96]{1,0:T(8,128)(2,1)S(1)}, u32[]{:S(2)}, u32[]{:S(2)}) collective-permute-start(bf16[32,96]{1,0:T(8,128)(2,1)S(1)} %get-tuple-element.19), channel_id=1, source_target_pairs={{0,2},{1,3},{2,0},{3,1},{4,6},{5,7},{6,4},{7,5},{8,10},{9,11},{10,... | collective-permute-start | bytes 18440 | tf_op jit(solution)/shard_map/ppermute | solution.py:265
  34.1 1.6 %collective-permute-done.8 = bf16[32,96]{1,0:T(8,128)(2,1)S(1)} collective-permute-done((bf16[32,96]{1,0:T(8,128)(2,1)S(1)}, bf16[32,96]{1,0:T(8,128)(2,1)S(1)}, u32[]{:S(2)}, u32[]{:S(2)}) %collective-permute-start.8) | collective-permute-done | bytes 6176 | tf_op jit(solution)/shard_map/ppermute | solution.py:265
  35.7 1.4 %collective-permute-done.9 = bf16[32,96]{1,0:T(8,128)(2,1)S(1)} collective-permute-done((bf16[32,96]{1,0:T(8,128)(2,1)S(1)}, bf16[32,96]{1,0:T(8,128)(2,1)S(1)}, u32[]{:S(2)}, u32[]{:S(2)}) %collective-permute-start.9) | collective-permute-done | bytes 6176 | tf_op jit(solution)/shard_map/ppermute | solution.py:265
  37.1 0.6 %add_bitcast_fusion = f32[96,32]{0,1:T(8,128)} fusion(bf16[32,96]{1,0:T(8,128)(2,1)S(1)} %collective-permute-done.9, bf16[32,96]{1,0:T(8,128)(2,1)S(1)} %collective-permute-done.8, bf16[32,96]{1,0:T(8,128)(2,1)S(1)} %collective-permute-done.7, bf16[128,96]{1,0:T(8,128)(2,1)S(1)} %collective-permute-done.6, s32[]{:T(128)S(6)} %select_n.12), kind=kLoop, calls=%fused_computation.5 | loop fusion | flops 21504 | bytes 36868 | tf_op jit(solution)/shard_map/transpose | solution.py:297
  (8 shorter events, 0.0 us)
Async XLA Ops:
  1.6 1.3 %collective-permute-start = (bf16[288,128]{1,0:T(8,128)(2,1)S(1)}, bf16[288,128]{1,0:T(8,128)(2,1)S(1)}, u32[]{:S(2)}, u32[]{:S(2)}) collective-permute-start(bf16[288,128]{1,0:T(8,128)(2,1)S(1)} %pad_maximum_fusion), channel_id=1, source_target_pairs={{0,0},{1,17},{2,10},{3,27},{4,4},{5,21},{6,14},{7,31},{8,8},{9,25}... | collective-permute-start | bytes 221192 | tf_op jit(solution)/shard_map/ppermute | solution.py:254
  2.9 16.6 %collective-permute-start.1 = (bf16[288,128]{1,0:T(8,128)(2,1)S(1)}, bf16[288,128]{1,0:T(8,128)(2,1)S(1)}, u32[]{:S(2)}, u32[]{:S(2)}) collective-permute-start(bf16[288,128]{1,0:T(8,128)(2,1)S(1)} %collective-permute-done.refs_0_), channel_id=1, source_target_pairs={{0,4},{4,0},{8,12},{12,8},{16,20},{20,16},{24,28},{28,24},{1,5},{5... | collective-permute-start | bytes 221192 | tf_op jit(solution)/shard_map/ppermute | solution.py:261
  6.7 6.6 %collective-permute-start.2 = (bf16[208,128]{1,0:T(8,128)(2,1)S(1)}, bf16[208,128]{1,0:T(8,128)(2,1)S(1)}, u32[]{:S(2)}, u32[]{:S(2)}) collective-permute-start(bf16[208,128]{1,0:T(8,128)(2,1)S(1)} %pad_maximum_fusion.1.refs_0_), channel_id=1, source_target_pairs={{0,1},{1,0},{2,3},{3,2},{4,5},{5,4},{6,7},{7,6},{8,9},{9,8},{10,11... | collective-permute-start | bytes 159752 | tf_op jit(solution)/shard_map/ppermute | solution.py:265
  10.9 4.7 %collective-permute-start.3 = (bf16[208,128]{1,0:T(8,128)(2,1)S(1)}, bf16[208,128]{1,0:T(8,128)(2,1)S(1)}, u32[]{:S(2)}, u32[]{:S(2)}) collective-permute-start(bf16[208,128]{1,0:T(8,128)(2,1)S(1)} %pad_maximum_fusion.1.refs_0_), channel_id=1, source_target_pairs={{0,2},{1,3},{2,0},{3,1},{4,6},{5,7},{6,4},{7,5},{8,10},{9,11},{10,... | collective-permute-start | bytes 159752 | tf_op jit(solution)/shard_map/ppermute | solution.py:265
  13.4 4.0 %collective-permute-start.4 = (bf16[208,128]{1,0:T(8,128)(2,1)S(1)}, bf16[208,128]{1,0:T(8,128)(2,1)S(1)}, u32[]{:S(2)}, u32[]{:S(2)}) collective-permute-start(bf16[208,128]{1,0:T(8,128)(2,1)S(1)} %pad_maximum_fusion.1.refs_0_), channel_id=1, source_target_pairs={{0,3},{1,2},{2,1},{3,0},{4,7},{5,6},{6,5},{7,4},{8,11},{9,10},{10,... | collective-permute-start | bytes 159752 | tf_op jit(solution)/shard_map/ppermute | solution.py:265
  17.4 1.6 %copy-start = (bf16[8192,128]{1,0:T(8,128)(2,1)S(1)}, bf16[8192,128]{1,0:T(8,128)(2,1)}, u32[]{:S(2)}) copy-start(bf16[8192,128]{1,0:T(8,128)(2,1)} %table_ref.1) | copy-start | bytes 6291460
  22.3 4.0 %collective-permute-start.5 = (bf16[128,96]{1,0:T(8,128)(2,1)S(1)}, bf16[128,96]{1,0:T(8,128)(2,1)S(1)}, u32[]{:S(2)}, u32[]{:S(2)}) collective-permute-start(bf16[128,96]{1,0:T(8,128)(2,1)S(1)} %shard_map.83.refs_6_), channel_id=1, source_target_pairs={{0,4},{4,0},{8,12},{12,8},{16,20},{20,16},{24,28},{28,24},{1,5},{5... | collective-permute-start | bytes 73736 | tf_op jit(solution)/shard_map/ppermute | solution.py:261
  26.3 0.7 %collective-permute-start.6 = (bf16[128,96]{1,0:T(8,128)(2,1)S(1)}, bf16[128,96]{1,0:T(8,128)(2,1)S(1)}, u32[]{:S(2)}, u32[]{:S(2)}) collective-permute-start(bf16[128,96]{1,0:T(8,128)(2,1)S(1)} %add_convert_fusion), channel_id=1, source_target_pairs={{0,0},{1,17},{2,10},{3,27},{4,4},{5,21},{6,14},{7,31},{8,8},{9,25}... | collective-permute-start | bytes 73736 | tf_op jit(solution)/shard_map/ppermute | solution.py:254
  27.0 7.0 %collective-permute-start.7 = (bf16[32,96]{1,0:T(8,128)(2,1)S(1)}, bf16[32,96]{1,0:T(8,128)(2,1)S(1)}, u32[]{:S(2)}, u32[]{:S(2)}) collective-permute-start(bf16[32,96]{1,0:T(8,128)(2,1)S(1)} %get-tuple-element.17), channel_id=1, source_target_pairs={{0,1},{1,0},{2,3},{3,2},{4,5},{5,4},{6,7},{7,6},{8,9},{9,8},{10,11... | collective-permute-start | bytes 18440 | tf_op jit(solution)/shard_map/ppermute | solution.py:265
  31.9 3.8 %collective-permute-start.8 = (bf16[32,96]{1,0:T(8,128)(2,1)S(1)}, bf16[32,96]{1,0:T(8,128)(2,1)S(1)}, u32[]{:S(2)}, u32[]{:S(2)}) collective-permute-start(bf16[32,96]{1,0:T(8,128)(2,1)S(1)} %get-tuple-element.19), channel_id=1, source_target_pairs={{0,2},{1,3},{2,0},{3,1},{4,6},{5,7},{6,4},{7,5},{8,10},{9,11},{10,... | collective-permute-start | bytes 18440 | tf_op jit(solution)/shard_map/ppermute | solution.py:265
  34.1 3.1 %collective-permute-start.9 = (bf16[32,96]{1,0:T(8,128)(2,1)S(1)}, bf16[32,96]{1,0:T(8,128)(2,1)S(1)}, u32[]{:S(2)}, u32[]{:S(2)}) collective-permute-start(bf16[32,96]{1,0:T(8,128)(2,1)S(1)} %get-tuple-element.18), channel_id=1, source_target_pairs={{0,3},{1,2},{2,1},{3,0},{4,7},{5,6},{6,5},{7,4},{8,11},{9,10},{10,... | collective-permute-start | bytes 18440 | tf_op jit(solution)/shard_map/ppermute | solution.py:265
where the time goes:
time: 38.1 us; the launch traced here: 37.8 us
  starting transfers between devices  18.6 us (49%)
  waiting for transfers between devices  7.72 us (20%)
  Pallas kernels  6.09 us (16%)
  other arithmetic  3.62 us (10%)
  local copies, waits for them, and re-layouts  1.6 us (4%)
    ppermute x6, starting transfers between devices, across(): return lax.ppermute(value, 'hid', pairs)  13.7 us
    ppermute x6, waiting for transfers between devices, across(): return lax.ppermute(value, 'hid', pairs)  7.1 us
    pallas_call x2, Pallas kernels, score_source(): pl.pallas_call(functools.partial(score_kernel, shard_rows, digits, tile_q...  5.59 us
    ppermute x2, starting transfers between devices, near(): return lax.ppermute(value, 'blk', pairs)  3.63 us
    unnamed x2, local copies, waits for them, and re-layouts  1.59 us
    ppermute x2, starting transfers between devices, far(): return lax.ppermute(value, ('blk', 'hid'), pairs)  1.32 us
    convert_element_type x1, other arithmetic, shards(): (beam >> SHIFT * d & 2 ** SHIFT - 1).astype(queries.dtype)  0.81 us
  transfers between devices with their start and end apart: 10, of which 5 were waited for; matrix products, arithmetic and copies ran while one was open for 4% of the time, Pallas kernels for 9%

commit v1 on v0

--- a/solution.py
+++ b/solution.py
@@ -20,52 +20,84 @@
 VMEM = pl.BlockSpec(memory_space=pltpu.VMEM)
 
 
-def prepare_kernel(part, table_ref, *refs):
-    packs = refs[:-5]
-    wide_ref, mix_ref, first_ref, column_ref, bias_ref = refs[-5:]
-    feat = table_ref.shape[1]
-
-    @pl.when(pl.program_id(0) == 0)
-    def _():
-        stacked = [
-            jnp.concatenate([p[i * part : (i + 1) * part, :] for p in packs], axis=0)
-            for i in range(3)
-        ]
-        first_ref[...] = stacked[0].T
-        mix_ref[0:feat, :] = stacked[1].T
-        mix_ref[feat:, :] = stacked[2].T
-        ends = [p[3 * part :, :].astype(jnp.float32) for p in packs]
-        out_row = jnp.concatenate([e[0:1, 0:part] for e in ends], axis=1)
-        bias = jnp.concatenate([e[1:2, 0:part] for e in ends], axis=1)
-        column_ref[...] = (
-            jnp.broadcast_to(out_row, (feat, out_row.shape[1])).T.astype(jnp.bfloat16)
-        )
-        bias_ref[...] = jnp.broadcast_to(bias, bias_ref.shape)
-
+def compose_kernel(digits, query_ref, beam_ref, message_ref):
+    feat = query_ref.shape[1]
+    width = beam_ref.shape[1]
+    message_ref[:, 0:feat] = query_ref[...]
+    ids = beam_ref[...]
+    for d in range(digits):
+        digit = (ids >> (SHIFT * (digits - 1 - d))) & (2**SHIFT - 1)
+        begin = feat + d * width
+        message_ref[:, begin : begin + width] = digit.astype(jnp.float32).astype(jnp.bfloat16)
+
+
+def compose(queries, beam, digits):
+    rows, feat = queries.shape
+    width = beam.shape[1]
+    return pl.pallas_call(
+        functools.partial(compose_kernel, digits),
+        in_specs=[VMEM, VMEM],
+        out_specs=VMEM,
+        out_shape=jax.ShapeDtypeStruct((rows, feat + digits * width), queries.dtype),
+        compiler_params=pltpu.CompilerParams(vmem_limit_bytes=60 * 2**20),
+    )(queries, beam)
+
+
+def widen_kernel(table_ref, wide_ref):
     wide_ref[...] = table_ref[...].astype(jnp.float32)
 
 
-def prepare(table, packs):
+def widen(table):
     rows, width = table.shape
     block = min(rows, 2048)
+    spec = pl.BlockSpec((block, width), lambda i: (i, 0))
+    return pl.pallas_call(
+        widen_kernel,
+        grid=(rows // block,),
+        in_specs=[spec],
+        out_specs=spec,
+        out_shape=jax.ShapeDtypeStruct((rows, width), jnp.float32),
+        compiler_params=pltpu.CompilerParams(vmem_limit_bytes=12 * 2**20),
+        cost_estimate=pl.CostEstimate(flops=0, bytes_accessed=6 * rows * width, transcendentals=0),
+    )(table)
+
+
+def assemble_kernel(part, *refs):
+    packs = refs[:-4]
+    mix_ref, first_ref, column_ref, bias_ref = refs[-4:]
+    feat = first_ref.shape[0]
+    stacked = [
+        jnp.concatenate([p[i * part : (i + 1) * part, :] for p in packs], axis=0) for i in range(3)
+    ]
+    first_ref[...] = stacked[0].T
+    mix_ref[0:feat, :] = stacked[1].T
+    mix_ref[feat:, :] = stacked[2].T
+    ends = [p[3 * part :, :].astype(jnp.float32) for p in packs]
+    out_row = jnp.concatenate([e[0:1, 0:part] for e in ends], axis=1)
+    bias = jnp.concatenate([e[0:1, part : 2 * part] for e in ends], axis=1)
+    column_ref[...] = jnp.broadcast_to(out_row, (feat, out_row.shape[1])).T.astype(jnp.bfloat16)
+    bias_ref[...] = jnp.broadcast_to(bias, bias_ref.shape)
+
+
+def assemble(packs):
+    width = packs[0].shape[1]
     part = (packs[0].shape[0] - TAIL) // 3
     hidden = part * len(packs)
-    whole = lambda shape: pl.BlockSpec(shape, lambda i: (0, 0))
-    shapes = ((2 * width, hidden), (width, hidden), (hidden, width), (SUBLANES, hidden))
-    types = (jnp.bfloat16, jnp.bfloat16, jnp.bfloat16, jnp.float32)
     return pl.pallas_call(
-        functools.partial(prepare_kernel, part),
-        grid=(rows // block,),
-        in_specs=[pl.BlockSpec((block, width), lambda i: (i, 0))]
-        + [whole(packs[0].shape)] * len(packs),
-        out_specs=(pl.BlockSpec((block, width), lambda i: (i, 0)), *[whole(x) for x in shapes]),
+        functools.partial(assemble_kernel, part),
+        in_specs=[VMEM] * len(packs),
+        out_specs=(VMEM,) * 4,
         out_shape=(
-            jax.ShapeDtypeStruct((rows, width), jnp.float32),
-            *[jax.ShapeDtypeStruct(x, t) for x, t in zip(shapes, types)],
+            jax.ShapeDtypeStruct((2 * width, hidden), jnp.bfloat16),
+            jax.ShapeDtypeStruct((width, hidden), jnp.bfloat16),
+            jax.ShapeDtypeStruct((hidden, width), jnp.bfloat16),
+            jax.ShapeDtypeStruct((SUBLANES, hidden), jnp.float32),
         ),
-        compiler_params=pltpu.CompilerParams(vmem_limit_bytes=12 * 2**20),
-        cost_estimate=pl.CostEstimate(flops=0, bytes_accessed=6 * rows * width, transcendentals=0),
-    )(table, *packs)
+        compiler_params=pltpu.CompilerParams(vmem_limit_bytes=4 * 2**20),
+        cost_estimate=pl.CostEstimate(
+            flops=0, bytes_accessed=8 * width * hidden, transcendentals=0
+        ),
+    )(*packs)
 
 
 def score_kernel(shard_rows, digits, tile_queries, follows, *refs):
@@ -90,9 +122,10 @@
     tiles = rows // tile_queries
     limit = width // 2 // SLOT
 
-    ids = asked_ref[rows : 2 * rows, :].astype(jnp.int32)
-    for d in range(2, digits + 1):
-        ids = (ids << SHIFT) + asked_ref[d * rows : (d + 1) * rows, :].astype(jnp.int32)
+    ids = asked_ref[:, feat : feat + width].astype(jnp.int32)
+    for d in range(1, digits):
+        begin = feat + d * width
+        ids = (ids << SHIFT) + asked_ref[:, begin : begin + width].astype(jnp.int32)
     local = ids - lax.axis_index("blk") * shard_rows
     owned = (local >= 0) & (local < shard_rows)
     even = owned & ((local & 1) == 0)
@@ -123,7 +156,7 @@
     passes = (most + (SLOT - 1)) // SLOT
     need_ref[...] = jnp.where(word != 0, front, -1)
     key_ref[...] = jnp.where(owned, local, -4)
-    queries = asked_ref[0:rows, :]
+    queries = asked_ref[:, 0:feat]
     query_ref[...] = queries.astype(jnp.float32)
     start_ref[...] = (
         jnp.dot(queries, first_ref[...], preferred_element_type=jnp.float32) + bias_ref[0:1, :]
@@ -194,9 +227,9 @@
 
 def score_source(asked, rows, shard_rows, prepared, before):
     wide, mix, first, column, bias = prepared
-    feat = asked.shape[1]
+    feat = wide.shape[1]
     hidden, width = column.shape
-    digits = asked.shape[0] // rows - 1
+    digits = (asked.shape[1] - feat) // width
     tile_queries = next(n for n in (32, 24, 16, 8) if rows % n == 0)
     tile = tile_queries * KIDS
     lanes = -(-rows // LANES) * LANES
@@ -265,18 +298,15 @@
         return lax.ppermute(value, "hid", pairs)
 
     digits = -(-(groups * shard_rows - 1).bit_length() // SHIFT)
-    split = [
-        ((beam >> (SHIFT * d)) & (2**SHIFT - 1)).astype(queries.dtype)
-        for d in reversed(range(digits))
-    ]
-    first = far(jnp.concatenate([queries] + split, axis=0))
+    first = far(compose(queries, beam, digits))
 
     part = w_out.shape[0]
-    ends = jnp.stack([w_out, bias_hidden])
-    ends = jnp.pad(ends, ((0, TAIL - 2), (0, feat - part)))
+    ends = jnp.concatenate([w_out, bias_hidden])[None]
+    ends = jnp.pad(ends, ((0, TAIL - 1), (0, feat - 2 * part)))
     weights = jnp.concatenate([w_query.T, w_node.T, w_cross.T, ends], axis=0)
     packs = [weights] + [across(weights, step) for step in range(1, parts)]
-    prepared = prepare(node_table, packs)
+    wide = widen(node_table)
+    prepared = (wide, *assemble(packs))
 
     total, before = None, ()
     for turn in reversed(range(turns)):

time: 38.1 us -> 36.3 us (0.953)
  waiting for transfers between devices: 7.72 us -> 5.79 us
  other arithmetic: 3.62 us -> 2.13 us
  Pallas kernels: 6.09 us -> 7.54 us
    ppermute x6, waiting for transfers between devices: 7.1 us -> 5.18 us  [across(): return lax.ppermute(value, 'hid', pairs)]
    pallas_call x1 -> x3, Pallas kernels: 0.51 us -> 1.96 us  [the longest x1 1.47 us: compose(): pl.pallas_call(functools.partial(compose_kernel, digits), in_specs=[VMEM,...]
    ppermute x2, starting transfers between devices: 1.32 us -> 2.19 us  [far(): return lax.ppermute(value, ('blk', 'hid'), pairs)]
    convert_element_type x1 -> x0, other arithmetic: 0.81 us -> none  [shards(): (beam >> SHIFT * d & 2 ** SHIFT - 1).astype(queries.dtype)]
    broadcast_in_dim x0 -> x1, other arithmetic: none -> 0.75 us  [shards(): ends = jnp.concatenate([w_out, bias_hidden])[None]]
    concatenate x1 -> x0, other arithmetic: 0.75 us -> none  [shards(): first = far(jnp.concatenate([queries] + split, axis=0))]
    another operation x1 -> x0, other arithmetic: 0.68 us -> none  [shards(): ends = jnp.stack([w_out, bias_hidden])]
    ppermute x6, starting transfers between devices: 13.7 us -> 13 us  [across(): return lax.ppermute(value, 'hid', pairs)]
where the time goes in v1:
time: 36.3 us; the launch traced here: 35.9 us
  starting transfers between devices  18.8 us (52%)
  Pallas kernels  7.54 us (21%)
  waiting for transfers between devices  5.79 us (16%)
  other arithmetic  2.13 us (6%)
  local copies, waits for them, and re-layouts  1.6 us (4%)
    ppermute x6, starting transfers between devices, across(): return lax.ppermute(value, 'hid', pairs)  13 us
    pallas_call x2, Pallas kernels, score_source(): pl.pallas_call(functools.partial(score_kernel, shard_rows, digits, tile_q...  5.58 us
    ppermute x6, waiting for transfers between devices, across(): return lax.ppermute(value, 'hid', pairs)  5.18 us
    ppermute x2, starting transfers between devices, near(): return lax.ppermute(value, 'blk', pairs)  3.57 us
    ppermute x2, starting transfers between devices, far(): return lax.ppermute(value, ('blk', 'hid'), pairs)  2.19 us
    unnamed x2, local copies, waits for them, and re-layouts  1.59 us
    pallas_call x1, Pallas kernels, compose(): pl.pallas_call(functools.partial(compose_kernel, digits), in_specs=[VMEM,...  1.47 us
    concatenate x1, other arithmetic, shards(): weights = jnp.concatenate([w_query.T, w_node.T, w_cross.T, ends], axis=0)  0.76 us
  transfers between devices with their start and end apart: 10, of which 5 were waited for; matrix products, arithmetic and copies ran while one was open for 4% of the time, Pallas kernels for 9%

profile of v1, /device:TPU:0, one launch (start us, length us, event | category | flops | bytes accessed | tf_op | source)
XLA Modules:
  0.0 35.9 jit_solution(12424220886538810537)
XLA Ops:
  0.0 1.5 %shard_map.82 = bf16[96,384]{1,0:T(8,128)(2,1)} custom-call(bf16[96,128]{1,0:T(8,128)(2,1)} %query_ref.1, s32[96,128]{1,0:T(8,128)} %beam_ref.1), custom_call_target="tpu_custom_call" | custom-call | tf_op jit(solution)/shard_map/pallas_call | solution.py:37
  1.5 1.5 %collective-permute-start = (bf16[96,384]{1,0:T(8,128)(2,1)}, bf16[96,384]{1,0:T(8,128)(2,1)S(1)}, u32[]{:S(2)}, u32[]{:S(2)}) collective-permute-start(bf16[96,384]{1,0:T(8,128)(2,1)} %shard_map.82), channel_id=1, source_target_pairs={{0,0},{1,17},{2,10},{3,27},{4,4},{5,21},{6,14},{7,31},{8,8},{9,25}... | collective-permute-start | bytes 221192 | tf_op jit(solution)/shard_map/ppermute | solution.py:287
  3.0 0.7 %maximum_bitcast_fusion = bf16[1,128]{1,0:T(2,128)(2,1)S(1)} fusion(bf16[64]{0:T(256)(128)(2,1)} %param.14, bf16[64]{0:T(256)(128)(2,1)} %param.15), kind=kLoop, calls=%fused_computation.8 | loop fusion | flops 512 | bytes 512 | tf_op jit(solution)/shard_map/broadcast_in_dim | solution.py:304
  3.7 3.0 %collective-permute-start.1 = (bf16[96,384]{1,0:T(8,128)(2,1)S(1)}, bf16[96,384]{1,0:T(8,128)(2,1)S(1)}, u32[]{:S(2)}, u32[]{:S(2)}) collective-permute-start(bf16[96,384]{1,0:T(8,128)(2,1)S(1)} %collective-permute-done.refs_0_), channel_id=1, source_target_pairs={{0,4},{4,0},{8,12},{12,8},{16,20},{20,16},{24,28},{28,24},{1,5},{5... | collective-permute-start | bytes 221192 | tf_op jit(solution)/shard_map/ppermute | solution.py:294
  6.7 0.8 %fusion.1.refs_0_ = bf16[208,128]{1,0:T(8,128)(2,1)S(1)} fusion(bf16[1,128]{1,0:T(2,128)(2,1)S(1)} %maximum_bitcast_fusion, bf16[64,128]{1,0:T(8,128)(2,1)} %bitcast.7, bf16[64,128]{1,0:T(8,128)(2,1)} %bitcast.8, bf16[64,128]{1,0:T(8,128)(2,1)} %bitcast.9), kind=kLoop, calls=%fused_computation.3 | loop fusion | flops 266240 | bytes 102656 | tf_op jit(solution)/shard_map/concatenate | solution.py:306
  7.5 3.5 %collective-permute-start.2 = (bf16[208,128]{1,0:T(8,128)(2,1)S(1)}, bf16[208,128]{1,0:T(8,128)(2,1)S(1)}, u32[]{:S(2)}, u32[]{:S(2)}) collective-permute-start(bf16[208,128]{1,0:T(8,128)(2,1)S(1)} %fusion.1.refs_0_), channel_id=1, source_target_pairs={{0,1},{1,0},{2,3},{3,2},{4,5},{5,4},{6,7},{7,6},{8,9},{9,8},{10,11... | collective-permute-start | bytes 159752 | tf_op jit(solution)/shard_map/ppermute | solution.py:298
  11.0 2.5 %collective-permute-start.3 = (bf16[208,128]{1,0:T(8,128)(2,1)S(1)}, bf16[208,128]{1,0:T(8,128)(2,1)S(1)}, u32[]{:S(2)}, u32[]{:S(2)}) collective-permute-start(bf16[208,128]{1,0:T(8,128)(2,1)S(1)} %fusion.1.refs_0_), channel_id=1, source_target_pairs={{0,2},{1,3},{2,0},{3,1},{4,6},{5,7},{6,4},{7,5},{8,10},{9,11},{10,... | collective-permute-start | bytes 159752 | tf_op jit(solution)/shard_map/ppermute | solution.py:298
  13.5 0.0 collective-permute-start.4
  13.5 1.6 %copy-done = bf16[8192,128]{1,0:T(8,128)(2,1)S(1)} copy-done((bf16[8192,128]{1,0:T(8,128)(2,1)S(1)}, bf16[8192,128]{1,0:T(8,128)(2,1)}, u32[]{:S(2)}) %copy-start) | copy-done | bytes 2097176
  15.1 0.3 shard_map.83.refs_1_
  15.4 0.0 collective-permute-done.2.refs_1_
  15.4 0.2 collective-permute-done.3.refs_2_
  15.7 1.9 %collective-permute-done.4.refs_3_ = bf16[208,128]{1,0:T(8,128)(2,1)S(1)} collective-permute-done((bf16[208,128]{1,0:T(8,128)(2,1)S(1)}, bf16[208,128]{1,0:T(8,128)(2,1)S(1)}, u32[]{:S(2)}, u32[]{:S(2)}) %collective-permute-start.4) | collective-permute-done | bytes 53280 | tf_op jit(solution)/shard_map/ppermute | solution.py:298
  17.5 0.2 shard_map.84
  17.7 2.8 %shard_map.85.refs_6_ = bf16[128,96]{1,0:T(8,128)(2,1)S(1)} custom-call(bf16[96,384]{1,0:T(8,128)(2,1)S(1)} %collective-permute-done.1.refs_0_, f32[8192,128]{1,0:T(8,128)S(1)} %shard_map.83.refs_1_, bf16[256,256]{1,0:T(8,128)(2,1)S(1)} %get-tuple-element.9.refs_2_, bf16[128,256]{1,0:T(8,128)(2,1)S(1)} %get-tuple-element.10.refs_3_, ...), custom_call_target="tpu_custom_call" | custom-call | flops 301989888 | bytes 786432 | tf_op jit(solution)/shard_map/pallas_call | solution.py:236
  20.5 0.6 %collective-permute-start.5 = (bf16[128,96]{1,0:T(8,128)(2,1)S(1)}, bf16[128,96]{1,0:T(8,128)(2,1)S(1)}, u32[]{:S(2)}, u32[]{:S(2)}) collective-permute-start(bf16[128,96]{1,0:T(8,128)(2,1)S(1)} %shard_map.85.refs_6_), channel_id=1, source_target_pairs={{0,4},{4,0},{8,12},{12,8},{16,20},{20,16},{24,28},{28,24},{1,5},{5... | collective-permute-start | bytes 73736 | tf_op jit(solution)/shard_map/ppermute | solution.py:294
  21.1 2.8 %shard_map.86 = bf16[128,96]{1,0:T(8,128)(2,1)S(1)} custom-call(bf16[96,384]{1,0:T(8,128)(2,1)S(1)} %collective-permute-done.refs_0_, f32[8192,128]{1,0:T(8,128)S(1)} %shard_map.83.refs_1_, bf16[256,256]{1,0:T(8,128)(2,1)S(1)} %get-tuple-element.9.refs_2_, bf16[128,256]{1,0:T(8,128)(2,1)S(1)} %get-tuple-element.10.refs_3_, ...), custom_call_target="tpu_custom_call" | custom-call | flops 301989888 | bytes 786432 | tf_op jit(solution)/shard_map/pallas_call | solution.py:236
  23.9 0.6 %collective-permute-done.5 = bf16[128,96]{1,0:T(8,128)(2,1)S(1)} collective-permute-done((bf16[128,96]{1,0:T(8,128)(2,1)S(1)}, bf16[128,96]{1,0:T(8,128)(2,1)S(1)}, u32[]{:S(2)}, u32[]{:S(2)}) %collective-permute-start.5) | collective-permute-done | bytes 24608 | tf_op jit(solution)/shard_map/ppermute | solution.py:294
  24.5 0.7 %collective-permute-start.6 = (bf16[128,96]{1,0:T(8,128)(2,1)S(1)}, bf16[128,96]{1,0:T(8,128)(2,1)S(1)}, u32[]{:S(2)}, u32[]{:S(2)}) collective-permute-start(bf16[128,96]{1,0:T(8,128)(2,1)S(1)} %add_convert_fusion), channel_id=1, source_target_pairs={{0,0},{1,17},{2,10},{3,27},{4,4},{5,21},{6,14},{7,31},{8,8},{9,25}... | collective-permute-start | bytes 73736 | tf_op jit(solution)/shard_map/ppermute | solution.py:287
  25.2 4.9 %collective-permute-start.7 = (bf16[32,96]{1,0:T(8,128)(2,1)S(1)}, bf16[32,96]{1,0:T(8,128)(2,1)S(1)}, u32[]{:S(2)}, u32[]{:S(2)}) collective-permute-start(bf16[32,96]{1,0:T(8,128)(2,1)S(1)} %get-tuple-element.13), channel_id=1, source_target_pairs={{0,1},{1,0},{2,3},{3,2},{4,5},{5,4},{6,7},{7,6},{8,9},{9,8},{10,11... | collective-permute-start | bytes 18440 | tf_op jit(solution)/shard_map/ppermute | solution.py:298
  30.1 2.1 %collective-permute-start.8 = (bf16[32,96]{1,0:T(8,128)(2,1)S(1)}, bf16[32,96]{1,0:T(8,128)(2,1)S(1)}, u32[]{:S(2)}, u32[]{:S(2)}) collective-permute-start(bf16[32,96]{1,0:T(8,128)(2,1)S(1)} %get-tuple-element.15), channel_id=1, source_target_pairs={{0,2},{1,3},{2,0},{3,1},{4,6},{5,7},{6,4},{7,5},{8,10},{9,11},{10,... | collective-permute-start | bytes 18440 | tf_op jit(solution)/shard_map/ppermute | solution.py:298
  32.3 1.6 %collective-permute-done.8 = bf16[32,96]{1,0:T(8,128)(2,1)S(1)} collective-permute-done((bf16[32,96]{1,0:T(8,128)(2,1)S(1)}, bf16[32,96]{1,0:T(8,128)(2,1)S(1)}, u32[]{:S(2)}, u32[]{:S(2)}) %collective-permute-start.8) | collective-permute-done | bytes 6176 | tf_op jit(solution)/shard_map/ppermute | solution.py:298
  33.9 1.4 %collective-permute-done.9 = bf16[32,96]{1,0:T(8,128)(2,1)S(1)} collective-permute-done((bf16[32,96]{1,0:T(8,128)(2,1)S(1)}, bf16[32,96]{1,0:T(8,128)(2,1)S(1)}, u32[]{:S(2)}, u32[]{:S(2)}) %collective-permute-start.9) | collective-permute-done | bytes 6176 | tf_op jit(solution)/shard_map/ppermute | solution.py:298
  35.3 0.6 %add_bitcast_fusion = f32[96,32]{0,1:T(8,128)} fusion(bf16[32,96]{1,0:T(8,128)(2,1)S(1)} %collective-permute-done.9, bf16[32,96]{1,0:T(8,128)(2,1)S(1)} %collective-permute-done.8, bf16[32,96]{1,0:T(8,128)(2,1)S(1)} %collective-permute-done.7, bf16[128,96]{1,0:T(8,128)(2,1)S(1)} %collective-permute-done.6, s32[]{:T(128)S(6)} %select_n.12), kind=kLoop, calls=%fused_computation.4 | loop fusion | flops 21504 | bytes 36868 | tf_op jit(solution)/shard_map/transpose | solution.py:327
  (8 shorter events, 0.0 us)
Async XLA Ops:
  1.5 2.3 %collective-permute-start = (bf16[96,384]{1,0:T(8,128)(2,1)}, bf16[96,384]{1,0:T(8,128)(2,1)S(1)}, u32[]{:S(2)}, u32[]{:S(2)}) collective-permute-start(bf16[96,384]{1,0:T(8,128)(2,1)} %shard_map.82), channel_id=1, source_target_pairs={{0,0},{1,17},{2,10},{3,27},{4,4},{5,21},{6,14},{7,31},{8,8},{9,25}... | collective-permute-start | bytes 221192 | tf_op jit(solution)/shard_map/ppermute | solution.py:287
  3.7 14.0 %collective-permute-start.1 = (bf16[96,384]{1,0:T(8,128)(2,1)S(1)}, bf16[96,384]{1,0:T(8,128)(2,1)S(1)}, u32[]{:S(2)}, u32[]{:S(2)}) collective-permute-start(bf16[96,384]{1,0:T(8,128)(2,1)S(1)} %collective-permute-done.refs_0_), channel_id=1, source_target_pairs={{0,4},{4,0},{8,12},{12,8},{16,20},{20,16},{24,28},{28,24},{1,5},{5... | collective-permute-start | bytes 221192 | tf_op jit(solution)/shard_map/ppermute | solution.py:294
  7.5 7.9 %collective-permute-start.2 = (bf16[208,128]{1,0:T(8,128)(2,1)S(1)}, bf16[208,128]{1,0:T(8,128)(2,1)S(1)}, u32[]{:S(2)}, u32[]{:S(2)}) collective-permute-start(bf16[208,128]{1,0:T(8,128)(2,1)S(1)} %fusion.1.refs_0_), channel_id=1, source_target_pairs={{0,1},{1,0},{2,3},{3,2},{4,5},{5,4},{6,7},{7,6},{8,9},{9,8},{10,11... | collective-permute-start | bytes 159752 | tf_op jit(solution)/shard_map/ppermute | solution.py:298
  11.0 4.7 %collective-permute-start.3 = (bf16[208,128]{1,0:T(8,128)(2,1)S(1)}, bf16[208,128]{1,0:T(8,128)(2,1)S(1)}, u32[]{:S(2)}, u32[]{:S(2)}) collective-permute-start(bf16[208,128]{1,0:T(8,128)(2,1)S(1)} %fusion.1.refs_0_), channel_id=1, source_target_pairs={{0,2},{1,3},{2,0},{3,1},{4,6},{5,7},{6,4},{7,5},{8,10},{9,11},{10,... | collective-permute-start | bytes 159752 | tf_op jit(solution)/shard_map/ppermute | solution.py:298
  13.5 4.0 %collective-permute-start.4 = (bf16[208,128]{1,0:T(8,128)(2,1)S(1)}, bf16[208,128]{1,0:T(8,128)(2,1)S(1)}, u32[]{:S(2)}, u32[]{:S(2)}) collective-permute-start(bf16[208,128]{1,0:T(8,128)(2,1)S(1)} %fusion.1.refs_0_), channel_id=1, source_target_pairs={{0,3},{1,2},{2,1},{3,0},{4,7},{5,6},{6,5},{7,4},{8,11},{9,10},{10,... | collective-permute-start | bytes 159752 | tf_op jit(solution)/shard_map/ppermute | solution.py:298
  13.5 1.6 %copy-start = (bf16[8192,128]{1,0:T(8,128)(2,1)S(1)}, bf16[8192,128]{1,0:T(8,128)(2,1)}, u32[]{:S(2)}) copy-start(bf16[8192,128]{1,0:T(8,128)(2,1)} %table_ref.1) | copy-start | bytes 6291460
  20.5 4.0 %collective-permute-start.5 = (bf16[128,96]{1,0:T(8,128)(2,1)S(1)}, bf16[128,96]{1,0:T(8,128)(2,1)S(1)}, u32[]{:S(2)}, u32[]{:S(2)}) collective-permute-start(bf16[128,96]{1,0:T(8,128)(2,1)S(1)} %shard_map.85.refs_6_), channel_id=1, source_target_pairs={{0,4},{4,0},{8,12},{12,8},{16,20},{20,16},{24,28},{28,24},{1,5},{5... | collective-permute-start | bytes 73736 | tf_op jit(solution)/shard_map/ppermute | solution.py:294
  24.5 0.7 %collective-permute-start.6 = (bf16[128,96]{1,0:T(8,128)(2,1)S(1)}, bf16[128,96]{1,0:T(8,128)(2,1)S(1)}, u32[]{:S(2)}, u32[]{:S(2)}) collective-permute-start(bf16[128,96]{1,0:T(8,128)(2,1)S(1)} %add_convert_fusion), channel_id=1, source_target_pairs={{0,0},{1,17},{2,10},{3,27},{4,4},{5,21},{6,14},{7,31},{8,8},{9,25}... | collective-permute-start | bytes 73736 | tf_op jit(solution)/shard_map/ppermute | solution.py:287
  25.2 7.0 %collective-permute-start.7 = (bf16[32,96]{1,0:T(8,128)(2,1)S(1)}, bf16[32,96]{1,0:T(8,128)(2,1)S(1)}, u32[]{:S(2)}, u32[]{:S(2)}) collective-permute-start(bf16[32,96]{1,0:T(8,128)(2,1)S(1)} %get-tuple-element.13), channel_id=1, source_target_pairs={{0,1},{1,0},{2,3},{3,2},{4,5},{5,4},{6,7},{7,6},{8,9},{9,8},{10,11... | collective-permute-start | bytes 18440 | tf_op jit(solution)/shard_map/ppermute | solution.py:298
  30.1 3.8 %collective-permute-start.8 = (bf16[32,96]{1,0:T(8,128)(2,1)S(1)}, bf16[32,96]{1,0:T(8,128)(2,1)S(1)}, u32[]{:S(2)}, u32[]{:S(2)}) collective-permute-start(bf16[32,96]{1,0:T(8,128)(2,1)S(1)} %get-tuple-element.15), channel_id=1, source_target_pairs={{0,2},{1,3},{2,0},{3,1},{4,6},{5,7},{6,4},{7,5},{8,10},{9,11},{10,... | collective-permute-start | bytes 18440 | tf_op jit(solution)/shard_map/ppermute | solution.py:298
  32.2 3.1 %collective-permute-start.9 = (bf16[32,96]{1,0:T(8,128)(2,1)S(1)}, bf16[32,96]{1,0:T(8,128)(2,1)S(1)}, u32[]{:S(2)}, u32[]{:S(2)}) collective-permute-start(bf16[32,96]{1,0:T(8,128)(2,1)S(1)} %get-tuple-element.14), channel_id=1, source_target_pairs={{0,3},{1,2},{2,1},{3,0},{4,7},{5,6},{6,5},{7,4},{8,11},{9,10},{10,... | collective-permute-start | bytes 18440 | tf_op jit(solution)/shard_map/ppermute | solution.py:298
